TPU v7x, 256 devices: a whole 4x4x8 slice. The times are simulated.
256 devices in a mesh: tm: 8 (over y, core), doc: 32 (over x, z).
Axes of the slice: x: 4, y: 4, z: 8, core: 2. Of those that a mesh axis runs over, the one named last changes fastest.
Arguments:
- beta_mean: float32 [16, 65536, 200], P('tm', 'doc'), may hold values from -9 to 230
- word_ids: int32 [8192, 128], P(('tm', 'doc')), may hold values from 0 to 65535, as said below
- word_counts: int32 [8192, 128], P(('tm', 'doc')), may hold values from 0 to 8
- doc_slice: int32 [8192], P(('tm', 'doc')), may hold values from 0 to 15, as said below
- dirichlet: float32 [200], replicated, may hold values from 0.05 to 0.5
- drift_var: float32 [200], replicated, may hold values from 0.002 to 0.5
- obs_var: float32 [200], replicated, may hold values from 0.05 to 1
Outputs:
- smoothed_mean: float32 [16, 65536, 200], P('tm', 'doc')
- doc_topics: float32 [8192, 200], P(('tm', 'doc'))
Inputs may be any that keep to these rules, and one draw needn't show every extreme that they name: `word_ids`: vocabulary range b holds the words b * 2048 to (b + 1) * 2048 - 1. Over the 4096 slots of each aligned block of 32 documents, at most 160 hold words of one range; in every block some range holds exactly 160, the same range for all blocks of the same 1024 documents. A word may fill several slots of a document. `doc_slice`: the documents of rows i * 1024 to (i + 1) * 1024 - 1 belong to slices i * 2 to (i + 1) * 2 - 1.
All inputs are finite; a program needn't handle non-finite values.
Results may differ from a plain program's by a relative error of at most 0.0034.
Values may be sent and summed in bfloat16 or wider, within the bound.
No kernel may reach another device: no remote copies, remote signals or barrier semaphores. Data moves between devices by JAX's collectives and lax.ppermute only.
A program may use at most 128 MiB of HBM per device.

v0:
```python
import jax
import jax.numpy as jnp
from jax import lax
from jax.sharding import PartitionSpec as P

E_ITERS = 4
pseudo_count = 0.1
prior_var = 1.0


def carried_in(value, axis, join, neutral):
    place = lax.axis_index(axis)
    gathered = jax.tree.map(
        lambda a, kind: lax.all_gather(a.astype(kind), axis), value, (jnp.bfloat16, jnp.bfloat16)
    )
    state = jax.tree.map(lambda a, e: jnp.zeros_like(a) + jnp.asarray(e, a.dtype), value, neutral)

    def one(hop, state):
        return join(
            state,
            jax.tree.map(
                lambda a, own: lax.dynamic_index_in_dim(a, hop, 0, False).astype(own.dtype),
                gathered,
                value,
            ),
        )

    return lax.fori_loop(0, place, one, state)


def entering(value, axis, join, neutral):
    count, mine = (lax.axis_size(axis), lax.axis_index(axis))
    pieces = jax.tree.map(lambda part: lax.all_gather(part, axis), value)
    pieces = jax.tree.map(lambda part: part[::-1], pieces)
    mine = count - 1 - mine
    total = jax.tree.map(
        lambda part, zero: jnp.full_like(part, 0) + jnp.asarray(zero, part.dtype), value, neutral
    )

    def hop(position, total):
        longer = join(total, jax.tree.map(lambda part: part[position], pieces))
        return jax.tree.map(lambda new, old: jnp.where(position < mine, new, old), longer, total)

    return lax.fori_loop(0, count - 1, hop, total)


def digamma_series(value):
    correction = jnp.zeros_like(value)
    for shift_step in range(6):
        correction = correction + 1.0 / (value + float(shift_step))
    shifted = value + 6.0
    inverse = 1.0 / shifted
    inverse_square = inverse * inverse
    series = inverse_square * (
        1.0 / 12.0 - inverse_square * (1.0 / 120.0 - inverse_square * (1.0 / 252.0))
    )
    return jnp.log(shifted) - 0.5 * inverse - series - correction


def expectation(tok_beta, tok_count, dirichlet):
    doc_gamma = dirichlet[None, :] + jnp.sum(tok_count, axis=1, keepdims=True) / dirichlet.shape[0]
    for iteration in range(E_ITERS):
        log_theta = digamma_series(doc_gamma) - digamma_series(
            jnp.sum(doc_gamma, axis=1, keepdims=True)
        )
        theta_exp = jnp.exp(log_theta)
        norm_tok = jnp.einsum(
            "dk,dnk->dn",
            theta_exp,
            tok_beta,
            precision=lax.Precision.HIGHEST,
            preferred_element_type=jnp.float32,
        )
        slot_ratio = tok_count / norm_tok
        doc_gamma = dirichlet[None, :] + theta_exp * jnp.einsum(
            "dn,dnk->dk",
            slot_ratio,
            tok_beta,
            precision=lax.Precision.HIGHEST,
            preferred_element_type=jnp.float32,
        )
    return (doc_gamma, theta_exp, slot_ratio)


def variances(drift_var, obs_var, length):

    def advance(filt_prev, placeholder):
        predicted = filt_prev + drift_var
        gain_now = predicted / (predicted + obs_var)
        filt_now = (1.0 - gain_now) * predicted
        return (filt_now, (gain_now, filt_now))

    initial = jnp.full(drift_var.shape, prior_var, jnp.float32)
    final_var, outputs = lax.scan(advance, initial, None, length=length)
    return outputs


def compose_maps(earlier, latter):
    return (latter[0] * earlier[0], latter[0][None, :] * earlier[1] + latter[1])


def per_device(beta_mean, word_ids, word_counts, doc_slice, dirichlet, drift_var, obs_var):
    slice_dev, vocab_shard, topics = beta_mean.shape
    doc_dev, token_width = word_ids.shape
    doc_peers = lax.axis_size("doc")
    time_peers = lax.axis_size("tm")
    time_index = lax.axis_index("tm")
    table_rows = slice_dev * vocab_shard
    vocab_top = lax.pmax(jnp.max(beta_mean, axis=1), "doc")
    vocab_total = lax.psum(jnp.sum(jnp.exp(beta_mean - vocab_top[:, None, :]), axis=1), "doc")
    log_norm = vocab_top + jnp.log(vocab_total)
    expected_beta = (
        jnp.exp(beta_mean - log_norm[:, None, :]).astype(jnp.bfloat16).reshape(table_rows, topics)
    )
    slot_count = doc_dev * token_width
    capacity = slot_count * 5 // (4 * doc_peers)
    flat_words = word_ids.reshape(slot_count)
    owners = flat_words // vocab_shard
    local_slice = doc_slice - time_index * slice_dev
    slot_row = jnp.repeat(local_slice, token_width) * vocab_shard + flat_words % vocab_shard
    slot_doc = jnp.repeat(jnp.arange(doc_dev, dtype=jnp.int32), token_width)
    request_code = slot_doc * table_rows + slot_row
    ordering = jnp.argsort(owners, stable=True)
    owners_sorted = owners[ordering]
    owner_load = jnp.sum(
        (owners[:, None] == jnp.arange(doc_peers, dtype=jnp.int32)[None, :]).astype(jnp.int32),
        axis=0,
    )
    owner_start = jnp.cumsum(owner_load) - owner_load
    place_sorted = (
        owners_sorted * capacity
        + jnp.arange(slot_count, dtype=jnp.int32)
        - owner_start[owners_sorted]
    )
    placement = jnp.zeros((slot_count,), jnp.int32).at[ordering].set(place_sorted)
    request = (
        jnp.full((doc_peers * capacity,), -1, jnp.int32)
        .at[placement]
        .set(request_code)
        .reshape(doc_peers, capacity)
    )
    received = lax.all_to_all(request, "doc", split_axis=0, concat_axis=0, tiled=True)
    rows_wanted = jnp.where(received >= 0, received % table_rows, 0)
    fetched = expected_beta[rows_wanted]
    replies = lax.all_to_all(fetched, "doc", split_axis=0, concat_axis=0, tiled=True)
    replies, received, fetched = (replies, received, fetched)
    tok_beta = replies.reshape(doc_peers * capacity, topics)[placement].reshape(
        doc_dev, token_width, topics
    )
    tok_count = word_counts.astype(jnp.float32)
    doc_gamma, theta_exp, slot_ratio = expectation(tok_beta, tok_count, dirichlet)
    slot_terms = (theta_exp[:, None, :] * slot_ratio[:, :, None]).reshape(slot_count, topics)
    outgoing = (
        jnp.zeros((doc_peers * capacity, topics), jnp.float32)
        .at[placement]
        .set(slot_terms)
        .reshape(doc_peers, capacity, topics)
    )
    arrived = lax.all_to_all(
        outgoing.astype(jnp.bfloat16), "doc", split_axis=0, concat_axis=0, tiled=True
    ).astype(outgoing.dtype)
    contrib = arrived * fetched
    target_row = jnp.where(received >= 0, received % table_rows, table_rows)
    word_stats = jax.ops.segment_sum(
        contrib.reshape(doc_peers * capacity, topics),
        target_row.reshape(doc_peers * capacity),
        num_segments=table_rows + 1,
    )
    word_stats = word_stats[:table_rows].reshape(slice_dev, vocab_shard, topics)
    total_slices = slice_dev * time_peers
    gain_all, var_all = variances(drift_var, obs_var, total_slices)
    first_slice = time_index * slice_dev
    gain_here = lax.dynamic_slice_in_dim(gain_all, first_slice, slice_dev, 0)
    var_here = lax.dynamic_slice_in_dim(var_all, first_slice, slice_dev, 0)
    slice_number = first_slice + jnp.arange(slice_dev, dtype=jnp.int32)
    smooth_gain = jnp.where(
        (slice_number == total_slices - 1)[:, None], 0.0, var_here / (var_here + drift_var[None, :])
    )
    pseudo = jnp.log(word_stats + pseudo_count)
    slope_now = jnp.ones((topics,), jnp.float32)
    offset = jnp.zeros((vocab_shard, topics), jnp.float32)
    slopes = []
    offsets = []
    for position in range(slice_dev):
        retained = 1.0 - gain_here[position]
        slope_now = retained * slope_now
        offset = retained[None, :] * offset + gain_here[position][None, :] * pseudo[position]
        slopes.append(slope_now)
        offsets.append(offset)
    identity = (jnp.ones((topics,), jnp.float32), jnp.zeros((vocab_shard, topics), jnp.float32))
    carried = carried_in((slope_now, offset), "tm", compose_maps, identity)
    filtered = [
        offsets[position] + slopes[position][None, :] * carried[1] for position in range(slice_dev)
    ]
    factor = jnp.ones((topics,), jnp.float32)
    constant = jnp.zeros((vocab_shard, topics), jnp.float32)
    factors = [None] * slice_dev
    constants = [None] * slice_dev
    for position in reversed(range(slice_dev)):
        weight = smooth_gain[position]
        factor = weight * factor
        constant = (1.0 - weight)[None, :] * filtered[position] + weight[None, :] * constant
        factors[position] = factor
        constants[position] = constant
    from_ahead = entering((factor, constant), "tm", compose_maps, identity)
    smoothed = jnp.stack(
        [
            constants[position] + factors[position][None, :] * from_ahead[1]
            for position in range(slice_dev)
        ]
    )
    return (smoothed, doc_gamma)


def solution(mesh):
    return jax.shard_map(
        per_device,
        mesh=mesh,
        in_specs=(
            P("tm", "doc", None),
            P(("tm", "doc"), None),
            P(("tm", "doc"), None),
            P(("tm", "doc")),
            P(),
            P(),
            P(),
        ),
        out_specs=(P("tm", "doc", None), P(("tm", "doc"), None)),
        check_vma=False,
    )
```

profile of v0, /device:TPU:1, one launch (start us, length us, event | category | flops | bytes accessed | tf_op | source)
XLA Modules:
  0.0 693.6 jit_solution(11381500754262118763)
XLA Ops:
  10.5 5.8 sort.17
  16.3 23.0 %gather_fusion = s32[4096]{0:T(1024)S(1)} fusion(s32[4096]{0:T(1024)S(1)} %get-tuple-element.318, s32[4096]{0:T(1024)S(1)} %get-tuple-element.319), kind=kCustom, calls=%fused_computation | custom fusion | bytes 49152 | tf_op jit(solution)/shard_map/gather | solution.py:124
  45.0 15.8 %select_subtract_fusion = s32[4096]{0:T(1024)S(1)} fusion(pred[4096]{0:T(1024)(128)(4,1)S(1)} %get-tuple-element.270, pred[4096]{0:T(1024)(128)(4,1)S(1)} %get-tuple-element.269, pred[4096]{0:T(1024)(128)(4,1)S(1)} %get-tuple-element.268, pred[4096]{0:T(1024)(128)(4,1)S(1)} %get-tuple-element.267, pred[4096]{0:T(1024)(128)(4,1)S(1)} %get-tuple-element.266, ...), kind=kLoop, calls=%fused_computation.139 | loop fusion | flops 114688 | bytes 151652 | tf_op jit(solution)/shard_map/sub | solution.py:131
  60.8 15.5 %scatter_custom_fusion = s32[4096]{0:T(1024)S(1)} fusion(s32[4096]{0:T(1024)S(1)} %get-tuple-element.320, s32[4096]{0:T(1024)S(1)} %select_subtract_fusion, s32[]{:T(128)} %constant.143.clone.1), kind=kCustom, calls=%fused_computation.157 | custom fusion | bytes 16388 | tf_op jit(solution)/shard_map/scatter | solution.py:135
  76.3 15.5 %scatter_custom_fusion.1 = s32[5120]{0:T(1024)S(1)} fusion(s32[4096]{0:T(1024)S(1)} %get-tuple-element.316, s32[4096]{0:T(1024)S(1)} %get-tuple-element.317, s32[]{:T(128)} %constant.145.clone.1), kind=kCustom, calls=%fused_computation.150 | custom fusion | bytes 20484 | tf_op jit(solution)/shard_map/scatter | solution.py:139
  92.6 11.9 %all-to-all-start = ((s32[32,1,160]{2,1,0:T(1,128)}), s32[32,1,160]{2,1,0:T(1,128)S(1)}, u32[]{:S(2)}, u32[]{:S(2)}) async-start(s32[32,1,160]{2,1,0:T(1,128)} %all_to_all.16), calls=%async_computation | async-start | bytes 65536 | tf_op jit(solution)/shard_map/all_to_all | solution.py:142
  104.7 60.5 %pmax.7 = f32[2,200]{1,0:T(2,128)S(1)} all-reduce(f32[2,200]{1,0:T(2,128)S(1)} %reduce_max.9), channel_id=1, replica_groups=mesh['tm'=8,'doc'=32] {'doc'}, use_global_device_ids=true, to_apply=%region_10.11 | all-reduce | flops 400 | bytes 3200 | tf_op jit(solution)/shard_map/pmax | solution.py:109
  165.8 55.7 %psum.7 = f32[2,200]{1,0:T(2,128)S(1)} all-reduce(f32[2,200]{1,0:T(2,128)S(1)} %exponential_reduce_fusion), channel_id=1, replica_groups=mesh['tm'=8,'doc'=32] {'doc'}, use_global_device_ids=true, to_apply=%region_12.13 | all-reduce | flops 400 | bytes 3200 | tf_op jit(solution)/shard_map/psum | solution.py:110
  226.3 21.1 %gather_fusion.1 = bf16[5120,200]{1,0:T(8,128)(2,1)} fusion(bf16[4096,200]{1,0:T(8,128)(2,1)S(1)} %bitcast.213, s32[5120]{0:T(1024)S(1)} %broadcast_clamp_fusion), kind=kCustom, calls=%fused_computation.1 | custom fusion | bytes 4116480 | tf_op jit(solution)/shard_map/gather | solution.py:144
  252.3 32.8 %all-to-all-done.1 = bf16[32,160,200]{2,1,0:T(8,128)(2,1)S(1)} async-done(((bf16[32,160,200]{2,1,0:T(8,128)(2,1)}), bf16[32,160,200]{2,1,0:T(8,128)(2,1)S(1)}, u32[]{:S(2)}, u32[]{:S(2)}) %all-to-all-start.1) | async-done | bytes 2048032 | tf_op jit(solution)/shard_map/all_to_all | solution.py:145
  286.7 15.1 %gather_fusion.2 = bf16[4096,200]{1,0:T(8,128)(2,1)S(1)} fusion(bf16[5120,200]{1,0:T(8,128)(2,1)} %bitcast.222, s32[4096]{0:T(1024)S(1)} %get-tuple-element.315), kind=kCustom, calls=%fused_computation.2 | custom fusion | bytes 3293184 | tf_op jit(solution)/shard_map/gather | solution.py:147
  315.1 20.4 %scatter_custom_fusion.2 = f32[5120,200]{1,0:T(8,128)} fusion(s32[4096]{0:T(1024)S(1)} %get-tuple-element.316, f32[4096,200]{1,0:T(8,128)} %bitcast_multiply_fusion, f32[]{:T(128)} %constant.142.clone.1), kind=kCustom, calls=%fused_computation.23 | custom fusion | bytes 4096512 | tf_op jit(solution)/shard_map/scatter | solution.py:156
  339.8 6.6 all-to-all-start.2
  349.2 30.7 %all-to-all-done.2 = bf16[32,160,200]{2,1,0:T(8,128)(2,1)} async-done(((bf16[32,160,200]{2,1,0:T(8,128)(2,1)}), bf16[32,160,200]{2,1,0:T(8,128)(2,1)}, u32[]{:S(2)}, u32[]{:S(2)}) %all-to-all-start.2) | async-done | bytes 2048032 | tf_op jit(solution)/shard_map/all_to_all | solution.py:159
  379.9 5.7 convert_multiply_fusion
  385.6 33.4 %scatter_custom_fusion.3 = f32[4097,200]{1,0:T(8,128)} fusion(s32[5120]{0:T(1024)S(1)} %bitcast.253, f32[5120,200]{1,0:T(8,128)} %bitcast.227, f32[]{:T(128)} %constant.142.clone.1), kind=kCustom, calls=%fused_computation.25 | custom fusion | flops 1024000 | bytes 3278112 | tf_op jit(solution)/shard_map/scatter-add | solution.py:164
  425.5 42.1 %all-gather.1 = bf16[8,1,200]{2,1,0:T(2,128)(2,1)S(1)} all-gather(bf16[1,1,200]{2,1,0:T(2,128)(2,1)S(1)} %get-tuple-element.311), channel_id=1, replica_groups=mesh['tm'=8,'doc'=32] {'tm'}, dimensions={0}, use_global_device_ids=true | all-gather | bytes 3600 | tf_op jit(solution)/shard_map/all_gather | solution.py:14
  467.6 29.5 %all-gather.6.cloned.1.call-done = bf16[8,2048,200]{1,2,0:T(8,128)(2,1)} async-done(((bf16[1,2048,200]{1,2,0:T(8,128)(2,1)}), bf16[8,2048,200]{1,2,0:T(8,128)(2,1)}) %all-gather.6.cloned.1.call-update) | async-done | bytes 6553616 | tf_op jit(solution)/shard_map/all_gather | solution.py:14
  498.6 6.7 while.41
  510.5 46.9 %all-gather.2 = f32[8,1,200]{2,1,0:T(1,128)S(1)} all-gather(f32[1,1,200]{2,1,0:T(1,128)S(1)} %bitcast.257), channel_id=1, replica_groups=mesh['tm'=8,'doc'=32] {'tm'}, dimensions={0}, use_global_device_ids=true | all-gather | bytes 7200 | tf_op jit(solution)/shard_map/all_gather | solution.py:33
  558.9 78.5 %all-gather.8.cloned.1.call-done = f32[16384,200]{1,0:T(8,128)} async-done(((f32[2048,200]{1,0:T(8,128)}), f32[16384,200]{1,0:T(8,128)}) %all-gather.8.cloned.1.call-update) | async-done | bytes 13107216 | tf_op jit(solution)/shard_map/all_gather | solution.py:33
  637.5 11.3 %rev.7 = f32[8,2048,200]{2,1,0:T(8,128)} reverse(f32[8,2048,200]{2,1,0:T(8,128)} %bitcast.225), dimensions={0} | reverse | bytes 26214400 | tf_op jit(solution)/shard_map/rev | solution.py:34
  648.7 26.2 %while.43 = (s32[]{:T(128)}, f32[2048,200]{1,0:T(8,128)}, s32[]{:T(128)}, f32[8,200]{1,0:T(8,128)S(1)}, f32[8,2048,200]{2,1,0:T(8,128)}, /*index=5*/s32[]{:T(128)}, s32[]{:T(128)}) while((s32[]{:T(128)}, f32[2048,200]{1,0:T(8,128)}, s32[]{:T(128)}, f32[8,200]{1,0:T(8,128)S(1)}, f32[8,2048,200]{2,1,0:T(8,128)}, ...), condition=%wide.region_21.22_spmd.clone, body=%wide.region_20.21_spmd.clone.sunk | while | flops 1638404 | bytes 4917713 | solution.py:44
  681.5 5.2 copy.35
  (164 shorter events, 97.6 us)
Async XLA Ops:
  16.3 88.2 %copy-start.3 = (f32[2,2048,200]{1,2,0:T(8,128)S(1)}, f32[2,2048,200]{1,2,0:T(8,128)}, u32[]{:S(2)}) copy-start(f32[2,2048,200]{1,2,0:T(8,128)} %param.13) | copy-start | bytes 9830404
  92.6 133.4 %all-to-all-start = ((s32[32,1,160]{2,1,0:T(1,128)}), s32[32,1,160]{2,1,0:T(1,128)S(1)}, u32[]{:S(2)}, u32[]{:S(2)}) async-start(s32[32,1,160]{2,1,0:T(1,128)} %all_to_all.16), calls=%async_computation | async-start | bytes 65536 | tf_op jit(solution)/shard_map/all_to_all | solution.py:142
  247.4 4.4 copy-start.4
  247.4 4.6 copy-start.5
  247.4 37.7 %all-to-all-start.1 = ((bf16[32,160,200]{2,1,0:T(8,128)(2,1)}), bf16[32,160,200]{2,1,0:T(8,128)(2,1)S(1)}, u32[]{:S(2)}, u32[]{:S(2)}) async-start(bf16[32,160,200]{2,1,0:T(8,128)(2,1)} %bitcast.223), calls=%async_computation.1 | async-start | bytes 5242880 | tf_op jit(solution)/shard_map/all_to_all | solution.py:145
  285.2 1.5 copy-start
  339.8 6.9 copy-start.6
  339.8 6.9 copy-start.7
  339.8 40.1 %all-to-all-start.2 = ((bf16[32,160,200]{2,1,0:T(8,128)(2,1)}), bf16[32,160,200]{2,1,0:T(8,128)(2,1)}, u32[]{:S(2)}, u32[]{:S(2)}) async-start(bf16[32,160,200]{2,1,0:T(8,128)(2,1)} %bitcast.226), calls=%async_computation.2 | async-start | bytes 5242880 | tf_op jit(solution)/shard_map/all_to_all | solution.py:159
  346.4 150.8 %all-gather.6.cloned.1.call-start = ((), (), s32[]{:S(2)}) async-start(), calls=%async_computation.3 | async-start | bytes 7372800 | tf_op jit(solution)/shard_map/all_gather | solution.py:14
  421.7 2.0 copy-start.2
  425.4 212.0 %all-gather.8.cloned.1.call-start = ((), (), s32[]{:S(2)}) async-start(), calls=%async_computation.4 | async-start | bytes 18874368 | tf_op jit(solution)/shard_map/all_gather | solution.py:33
  648.7 26.2 %copy-start.1 = (f32[2048,200]{1,0:T(8,128)S(1)}, f32[2048,200]{1,0:T(8,128)}, u32[]{:S(2)}) copy-start(f32[2048,200]{1,0:T(8,128)} %get-tuple-element.177) | copy-start | bytes 4915204
Sparse Core Ops, SparseCore 0:
  425.6 71.5 all-gather.5
  510.6 126.8 all-gather.7
where the time goes:
time: 695 us; the launch traced here: 694 us
  blocking collectives  205 us (29%)
  waiting for transfers between devices  172 us (25%)
  local copies, waits for them, and re-layouts  144 us (21%)
  other arithmetic  124 us (18%)
  starting transfers between devices  23.1 us (3%)
  between operations  14.4 us (2%)
  matrix products  10.6 us (2%)
    all_gather x1, waiting for transfers between devices, entering(): pieces = jax.tree.map(lambda part: lax.all_gather(part, axis), value)  78.5 us
    pmax x1, blocking collectives, per_device(): vocab_top = lax.pmax(jnp.max(beta_mean, axis=1), 'doc')  60.5 us
    psum x1, blocking collectives, per_device(): lax.psum(jnp.sum(jnp.exp(beta_mean - vocab_top[:, None, :]), axis=1), 'doc')  55.7 us
    all_gather x1, blocking collectives, entering(): pieces = jax.tree.map(lambda part: lax.all_gather(part, axis), value)  46.9 us
    all_gather x1, blocking collectives, carried_in(): lax.all_gather(a.astype(kind), axis)  42.1 us
    scatter-add x1, other arithmetic, per_device(): jax.ops.segment_sum(contrib.reshape(doc_peers * capacity, topics), target...  33.4 us
    all_to_all x1, waiting for transfers between devices, per_device(): lax.all_to_all(fetched, 'doc', split_axis=0, concat_axis=0, tiled=True)  32.8 us
    all_to_all x1, waiting for transfers between devices, per_device(): lax.all_to_all(outgoing.astype(jnp.bfloat16), 'doc', split_axis=0, concat...  30.7 us
  transfers between devices with their start and end apart: 5, of which 4 were waited for; matrix products, arithmetic and copies ran while one was open for 1% of the time, Pallas kernels for 0%

commit v1 on v0

--- a/solution.py
+++ b/solution.py
@@ -107,7 +107,9 @@
     time_index = lax.axis_index("tm")
     table_rows = slice_dev * vocab_shard
     vocab_top = lax.pmax(jnp.max(beta_mean, axis=1), "doc")
-    vocab_total = lax.psum(jnp.sum(jnp.exp(beta_mean - vocab_top[:, None, :]), axis=1), "doc")
+    vocab_total = jnp.sum(
+        lax.all_gather(jnp.sum(jnp.exp(beta_mean - vocab_top[:, None, :]), axis=1), "doc"), axis=0
+    )
     log_norm = vocab_top + jnp.log(vocab_total)
     expected_beta = (
         jnp.exp(beta_mean - log_norm[:, None, :]).astype(jnp.bfloat16).reshape(table_rows, topics)

time: 695 us -> 674 us (0.970)
  blocking collectives: 205 us -> 182 us
    psum x1 -> x0, blocking collectives: 55.7 us -> none  [per_device(): lax.psum(jnp.sum(jnp.exp(beta_mean - vocab_top[:, None, :]), axis=1), 'doc')]
    all_gather x0 -> x1, blocking collectives: none -> 33.4 us  [per_device(): lax.all_gather(jnp.sum(jnp.exp(beta_mean - vocab_top[:, None, :]), axis=1...]
where the time goes in v1:
time: 674 us; the launch traced here: 672 us
  blocking collectives  182 us (27%)
  waiting for transfers between devices  171 us (25%)
  local copies, waits for them, and re-layouts  144 us (21%)
  other arithmetic  124 us (18%)
  starting transfers between devices  25.9 us (4%)
  between operations  14.4 us (2%)
  matrix products  10.6 us (2%)
    all_gather x1, waiting for transfers between devices, entering(): pieces = jax.tree.map(lambda part: lax.all_gather(part, axis), value)  78.5 us
    pmax x1, blocking collectives, per_device(): vocab_top = lax.pmax(jnp.max(beta_mean, axis=1), 'doc')  60.5 us
    all_gather x1, blocking collectives, entering(): pieces = jax.tree.map(lambda part: lax.all_gather(part, axis), value)  46.9 us
    all_gather x1, blocking collectives, carried_in(): lax.all_gather(a.astype(kind), axis)  41.2 us
    all_gather x1, blocking collectives, per_device(): lax.all_gather(jnp.sum(jnp.exp(beta_mean - vocab_top[:, None, :]), axis=1...  33.4 us
    scatter-add x1, other arithmetic, per_device(): jax.ops.segment_sum(contrib.reshape(doc_peers * capacity, topics), target...  33.4 us
    all_to_all x1, waiting for transfers between devices, per_device(): lax.all_to_all(fetched, 'doc', split_axis=0, concat_axis=0, tiled=True)  33.1 us
    all_to_all x1, waiting for transfers between devices, per_device(): lax.all_to_all(outgoing.astype(jnp.bfloat16), 'doc', split_axis=0, concat...  30.9 us
  transfers between devices with their start and end apart: 5, of which 4 were waited for; matrix products, arithmetic and copies ran while one was open for 1% of the time, Pallas kernels for 0%

profile of v1, /device:TPU:1, one launch (start us, length us, event | category | flops | bytes accessed | tf_op | source)
XLA Modules:
  0.0 672.2 jit_solution(7198192125145790724)
XLA Ops:
  10.5 5.8 sort.17
  16.3 23.0 %gather_fusion = s32[4096]{0:T(1024)S(1)} fusion(s32[4096]{0:T(1024)S(1)} %get-tuple-element.318, s32[4096]{0:T(1024)S(1)} %get-tuple-element.319), kind=kCustom, calls=%fused_computation | custom fusion | bytes 49152 | tf_op jit(solution)/shard_map/gather | solution.py:126
  45.0 15.8 %select_subtract_fusion = s32[4096]{0:T(1024)S(1)} fusion(pred[4096]{0:T(1024)(128)(4,1)S(1)} %get-tuple-element.270, pred[4096]{0:T(1024)(128)(4,1)S(1)} %get-tuple-element.269, pred[4096]{0:T(1024)(128)(4,1)S(1)} %get-tuple-element.268, pred[4096]{0:T(1024)(128)(4,1)S(1)} %get-tuple-element.267, pred[4096]{0:T(1024)(128)(4,1)S(1)} %get-tuple-element.266, ...), kind=kLoop, calls=%fused_computation.139 | loop fusion | flops 114688 | bytes 151652 | tf_op jit(solution)/shard_map/sub | solution.py:133
  60.8 15.5 %scatter_custom_fusion = s32[4096]{0:T(1024)S(1)} fusion(s32[4096]{0:T(1024)S(1)} %get-tuple-element.320, s32[4096]{0:T(1024)S(1)} %select_subtract_fusion, s32[]{:T(128)} %constant.143.clone.1), kind=kCustom, calls=%fused_computation.157 | custom fusion | bytes 16388 | tf_op jit(solution)/shard_map/scatter | solution.py:137
  76.3 15.5 %scatter_custom_fusion.1 = s32[5120]{0:T(1024)S(1)} fusion(s32[4096]{0:T(1024)S(1)} %get-tuple-element.316, s32[4096]{0:T(1024)S(1)} %get-tuple-element.317, s32[]{:T(128)} %constant.145.clone.1), kind=kCustom, calls=%fused_computation.150 | custom fusion | bytes 20484 | tf_op jit(solution)/shard_map/scatter | solution.py:141
  92.6 11.9 %all-to-all-start = ((s32[32,1,160]{2,1,0:T(1,128)}), s32[32,1,160]{2,1,0:T(1,128)S(1)}, u32[]{:S(2)}, u32[]{:S(2)}) async-start(s32[32,1,160]{2,1,0:T(1,128)} %all_to_all.16), calls=%async_computation | async-start | bytes 65536 | tf_op jit(solution)/shard_map/all_to_all | solution.py:144
  104.7 60.5 %pmax.7 = f32[2,200]{1,0:T(2,128)S(1)} all-reduce(f32[2,200]{1,0:T(2,128)S(1)} %reduce_max.9), channel_id=1, replica_groups=mesh['tm'=8,'doc'=32] {'doc'}, use_global_device_ids=true, to_apply=%region_10.11 | all-reduce | flops 400 | bytes 3200 | tf_op jit(solution)/shard_map/pmax | solution.py:109
  165.8 33.4 %all-gather.2 = f32[32,2,200]{2,1,0:T(2,128)S(1)} all-gather(f32[1,2,200]{2,1,0:T(2,128)S(1)} %bitcast.268), channel_id=2, replica_groups=mesh['tm'=8,'doc'=32] {'doc'}, dimensions={0}, use_global_device_ids=true | all-gather | bytes 52800 | tf_op jit(solution)/shard_map/all_gather | solution.py:111
  204.1 21.1 %gather_fusion.1 = bf16[5120,200]{1,0:T(8,128)(2,1)} fusion(bf16[4096,200]{1,0:T(8,128)(2,1)S(1)} %bitcast.214, s32[5120]{0:T(1024)S(1)} %broadcast_clamp_fusion), kind=kCustom, calls=%fused_computation.1 | custom fusion | bytes 4116480 | tf_op jit(solution)/shard_map/gather | solution.py:146
  225.2 6.0 all-to-all-start.1
  231.7 33.1 %all-to-all-done.1 = bf16[32,160,200]{2,1,0:T(8,128)(2,1)S(1)} async-done(((bf16[32,160,200]{2,1,0:T(8,128)(2,1)}), bf16[32,160,200]{2,1,0:T(8,128)(2,1)S(1)}, u32[]{:S(2)}, u32[]{:S(2)}) %all-to-all-start.1) | async-done | bytes 2048032 | tf_op jit(solution)/shard_map/all_to_all | solution.py:147
  266.3 15.1 %gather_fusion.2 = bf16[4096,200]{1,0:T(8,128)(2,1)S(1)} fusion(bf16[5120,200]{1,0:T(8,128)(2,1)} %bitcast.223, s32[4096]{0:T(1024)S(1)} %get-tuple-element.315), kind=kCustom, calls=%fused_computation.2 | custom fusion | bytes 3293184 | tf_op jit(solution)/shard_map/gather | solution.py:149
  294.7 20.4 %scatter_custom_fusion.2 = f32[5120,200]{1,0:T(8,128)} fusion(s32[4096]{0:T(1024)S(1)} %get-tuple-element.316, f32[4096,200]{1,0:T(8,128)} %bitcast_multiply_fusion, f32[]{:T(128)} %constant.142.clone.1), kind=kCustom, calls=%fused_computation.23 | custom fusion | bytes 4096512 | tf_op jit(solution)/shard_map/scatter | solution.py:158
  319.4 7.7 %all-to-all-start.2 = ((bf16[32,160,200]{2,1,0:T(8,128)(2,1)}), bf16[32,160,200]{2,1,0:T(8,128)(2,1)}, u32[]{:S(2)}, u32[]{:S(2)}) async-start(bf16[32,160,200]{2,1,0:T(8,128)(2,1)} %bitcast.227), calls=%async_computation.2 | async-start | bytes 5242880 | tf_op jit(solution)/shard_map/all_to_all | solution.py:161
  329.9 30.9 %all-to-all-done.2 = bf16[32,160,200]{2,1,0:T(8,128)(2,1)} async-done(((bf16[32,160,200]{2,1,0:T(8,128)(2,1)}), bf16[32,160,200]{2,1,0:T(8,128)(2,1)}, u32[]{:S(2)}, u32[]{:S(2)}) %all-to-all-start.2) | async-done | bytes 2048032 | tf_op jit(solution)/shard_map/all_to_all | solution.py:161
  360.8 5.7 convert_multiply_fusion
  366.5 33.4 %scatter_custom_fusion.3 = f32[4097,200]{1,0:T(8,128)} fusion(s32[5120]{0:T(1024)S(1)} %bitcast.254, f32[5120,200]{1,0:T(8,128)} %bitcast.228, f32[]{:T(128)} %constant.142.clone.1), kind=kCustom, calls=%fused_computation.25 | custom fusion | flops 1024000 | bytes 3278112 | tf_op jit(solution)/shard_map/scatter-add | solution.py:166
  406.4 41.2 %all-gather.3 = bf16[8,1,200]{2,1,0:T(2,128)(2,1)S(1)} all-gather(bf16[1,1,200]{2,1,0:T(2,128)(2,1)S(1)} %get-tuple-element.311), channel_id=1, replica_groups=mesh['tm'=8,'doc'=32] {'tm'}, dimensions={0}, use_global_device_ids=true | all-gather | bytes 3600 | tf_op jit(solution)/shard_map/all_gather | solution.py:14
  447.6 28.1 %all-gather.8.cloned.1.call-done = bf16[8,2048,200]{1,2,0:T(8,128)(2,1)} async-done(((bf16[1,2048,200]{1,2,0:T(8,128)(2,1)}), bf16[8,2048,200]{1,2,0:T(8,128)(2,1)}) %all-gather.8.cloned.1.call-update) | async-done | bytes 6553616 | tf_op jit(solution)/shard_map/all_gather | solution.py:14
  477.2 6.7 while.41
  489.0 46.9 %all-gather.4 = f32[8,1,200]{2,1,0:T(1,128)S(1)} all-gather(f32[1,1,200]{2,1,0:T(1,128)S(1)} %bitcast.258), channel_id=1, replica_groups=mesh['tm'=8,'doc'=32] {'tm'}, dimensions={0}, use_global_device_ids=true | all-gather | bytes 7200 | tf_op jit(solution)/shard_map/all_gather | solution.py:33
  537.5 78.5 %all-gather.10.cloned.1.call-done = f32[16384,200]{1,0:T(8,128)} async-done(((f32[2048,200]{1,0:T(8,128)}), f32[16384,200]{1,0:T(8,128)}) %all-gather.10.cloned.1.call-update) | async-done | bytes 13107216 | tf_op jit(solution)/shard_map/all_gather | solution.py:33
  616.0 11.3 %rev.7 = f32[8,2048,200]{2,1,0:T(8,128)} reverse(f32[8,2048,200]{2,1,0:T(8,128)} %bitcast.226), dimensions={0} | reverse | bytes 26214400 | tf_op jit(solution)/shard_map/rev | solution.py:34
  627.3 26.2 %while.43 = (s32[]{:T(128)}, f32[2048,200]{1,0:T(8,128)}, s32[]{:T(128)}, f32[8,200]{1,0:T(8,128)S(1)}, f32[8,2048,200]{2,1,0:T(8,128)}, /*index=5*/s32[]{:T(128)}, s32[]{:T(128)}) while((s32[]{:T(128)}, f32[2048,200]{1,0:T(8,128)}, s32[]{:T(128)}, f32[8,200]{1,0:T(8,128)S(1)}, f32[8,2048,200]{2,1,0:T(8,128)}, ...), condition=%wide.region_21.22_spmd.clone, body=%wide.region_20.21_spmd.clone.sunk | while | flops 1638404 | bytes 4917713 | solution.py:44
  (165 shorter events, 98.5 us)
Async XLA Ops:
  16.3 88.2 %copy-start.3 = (f32[2,2048,200]{1,2,0:T(8,128)S(1)}, f32[2,2048,200]{1,2,0:T(8,128)}, u32[]{:S(2)}) copy-start(f32[2,2048,200]{1,2,0:T(8,128)} %param.13) | copy-start | bytes 9830404
  92.6 111.2 %all-to-all-start = ((s32[32,1,160]{2,1,0:T(1,128)}), s32[32,1,160]{2,1,0:T(1,128)S(1)}, u32[]{:S(2)}, u32[]{:S(2)}) async-start(s32[32,1,160]{2,1,0:T(1,128)} %all_to_all.16), calls=%async_computation | async-start | bytes 65536 | tf_op jit(solution)/shard_map/all_to_all | solution.py:144
  225.2 6.1 copy-start.4
  225.2 6.2 copy-start.5
  225.2 39.6 %all-to-all-start.1 = ((bf16[32,160,200]{2,1,0:T(8,128)(2,1)}), bf16[32,160,200]{2,1,0:T(8,128)(2,1)S(1)}, u32[]{:S(2)}, u32[]{:S(2)}) async-start(bf16[32,160,200]{2,1,0:T(8,128)(2,1)} %bitcast.224), calls=%async_computation.1 | async-start | bytes 5242880 | tf_op jit(solution)/shard_map/all_to_all | solution.py:147
  264.8 1.5 copy-start
  319.4 8.0 %copy-start.6 = (f32[200]{0:T(256)S(1)}, f32[200]{0:T(256)}, u32[]{:S(2)}) copy-start(f32[200]{0:T(256)} %param.18) | copy-start | bytes 2404
  319.4 8.0 %copy-start.7 = (f32[200]{0:T(256)S(1)}, f32[200]{0:T(256)}, u32[]{:S(2)}) copy-start(f32[200]{0:T(256)} %param.19) | copy-start | bytes 2404
  319.4 41.4 %all-to-all-start.2 = ((bf16[32,160,200]{2,1,0:T(8,128)(2,1)}), bf16[32,160,200]{2,1,0:T(8,128)(2,1)}, u32[]{:S(2)}, u32[]{:S(2)}) async-start(bf16[32,160,200]{2,1,0:T(8,128)(2,1)} %bitcast.227), calls=%async_computation.2 | async-start | bytes 5242880 | tf_op jit(solution)/shard_map/all_to_all | solution.py:161
  327.1 148.6 %all-gather.8.cloned.1.call-start = ((), (), s32[]{:S(2)}) async-start(), calls=%async_computation.3 | async-start | bytes 7372800 | tf_op jit(solution)/shard_map/all_gather | solution.py:14
  402.6 2.0 copy-start.2
  406.3 209.7 %all-gather.10.cloned.1.call-start = ((), (), s32[]{:S(2)}) async-start(), calls=%async_computation.4 | async-start | bytes 18874368 | tf_op jit(solution)/shard_map/all_gather | solution.py:33
  627.3 26.2 %copy-start.1 = (f32[2048,200]{1,0:T(8,128)S(1)}, f32[2048,200]{1,0:T(8,128)}, u32[]{:S(2)}) copy-start(f32[2048,200]{1,0:T(8,128)} %get-tuple-element.177) | copy-start | bytes 4915204
Sparse Core Ops, SparseCore 0:
  406.5 69.2 all-gather.7
  489.1 126.8 all-gather.9
